TPU v7x, 32 devices: a whole 2x2x4 slice. The times are simulated.
32 devices in a mesh: kvh: 4 (over y, x), seq: 8 (over z, core).
Axes of the slice: x: 2, y: 2, z: 4, core: 2. Of those that a mesh axis runs over, the one named last changes fastest.
Arguments:
- queries: bfloat16 [4, 128, 128], P(None, 'kvh'), may hold values from -256 to 256
- keys: bfloat16 [4, 8, 1024, 128], P(None, 'kvh', 'seq'), may hold values from -6 to 6
- values: bfloat16 [4, 8, 1024, 128], P(None, 'kvh', 'seq'), may hold values from -6 to 6
- lengths: int32 [4, 8], P(None, 'seq'), may hold values from 2 to 128
- hidden_in: bfloat16 [4, 16384], P(None, ('kvh', 'seq')), may hold values from -10 to 10
- out_weight: bfloat16 [16384, 16384], P(('kvh', 'seq')), may hold values from -1 to 1
- norm_gain: bfloat16 [16384], replicated, may hold values from 0.3984375 to 1.59375
Outputs:
- attended: bfloat16 [4, 16384], P(None, ('kvh', 'seq'))
- normed: bfloat16 [4, 16384], P(None, ('kvh', 'seq'))
All inputs are finite; a program needn't handle non-finite values.
Results may differ from a plain program's by a relative error of at most 0.006.
Values may be sent and summed in bfloat16 or wider, within the bound.
A program may use at most 64 MiB of HBM per device.

v0:
```python
import jax
import jax.numpy as jnp
from jax import lax
from jax.sharding import PartitionSpec as P


def merged(shard, axis, combine):
    everything = jax.tree.map(lambda part: lax.all_gather(part, axis), shard)
    leading = jax.tree.map(lambda part: part[0], everything)

    def lap(k, so_far):
        return combine(so_far, jax.tree.map(lambda part: part[k], everything))

    return lax.fori_loop(1, lax.axis_size(axis), lap, leading)


def softmax_pair(first, second):
    highest = jnp.maximum(first[0], second[0])
    first_scale = jnp.exp(first[0] - highest)
    second_scale = jnp.exp(second[0] - highest)
    weight_total = first[1] * first_scale + second[1] * second_scale
    output_total = first[2] * first_scale[..., None] + second[2] * second_scale[..., None]
    return (highest, weight_total, output_total)


def body(queries, keys, values, lengths, hidden_in, out_weight, norm_gain):
    rows, heads_here, head_dim = queries.shape
    groups = keys.shape[1]
    positions = keys.shape[2]
    per_group = heads_here // groups
    query_grid = queries.reshape(rows, groups, per_group, head_dim)
    scores = jnp.einsum(
        "rkgd,rktd->rkgt", query_grid, keys, preferred_element_type=jnp.float32
    ) * head_dim ** (-0.5)
    valid = (jnp.arange(positions, dtype=jnp.int32)[None, :] < lengths)[:, None, None, :]
    peak_here = jnp.max(jnp.where(valid, scores, -jnp.inf), axis=-1)
    probs = jnp.exp(jnp.where(valid, scores - peak_here[..., None], -jnp.inf)).astype(jnp.bfloat16)
    weight_here = jnp.sum(probs, axis=-1, dtype=jnp.float32)
    partial_value = jnp.einsum("rkgt,rktd->rkgd", probs, values, preferred_element_type=jnp.float32)
    feature_width = heads_here * head_dim // lax.axis_size("seq")
    feature_start = lax.axis_index("seq") * feature_width
    highest, weight_total, output_total = merged(
        (peak_here, weight_here, partial_value), "seq", softmax_pair
    )
    whole_out = (output_total / weight_total[..., None]).reshape(rows, heads_here * head_dim)
    attention = lax.dynamic_slice_in_dim(whole_out, feature_start, feature_width, 1)
    attention = attention.astype(jnp.bfloat16)
    projected = jnp.dot(attention, out_weight, preferred_element_type=jnp.float32)
    slice_width = hidden_in.shape[1]
    slice_start = lax.axis_index(("kvh", "seq")) * slice_width
    gain_wide = norm_gain.astype(jnp.float32)
    projected_all = lax.psum(projected, ("kvh", "seq"))
    residual = lax.all_gather(hidden_in, ("kvh", "seq"), axis=1, tiled=True)
    stream_all = (residual.astype(jnp.float32) + projected_all).astype(jnp.bfloat16)
    stream_wide = stream_all.astype(jnp.float32)
    mean_square = jnp.mean(stream_wide * stream_wide, axis=1, keepdims=True)
    normed_all = (stream_wide * lax.rsqrt(mean_square + 1e-05) * gain_wide[None, :]).astype(
        jnp.bfloat16
    )
    attended = lax.dynamic_slice_in_dim(stream_all, slice_start, slice_width, 1)
    normed = lax.dynamic_slice_in_dim(normed_all, slice_start, slice_width, 1)
    return (attended, normed)


def solution(mesh):
    placed = (
        P(None, "kvh", None),
        P(None, "kvh", "seq", None),
        P(None, "kvh", "seq", None),
        P(None, "seq"),
        P(None, ("kvh", "seq")),
        P(("kvh", "seq"), None),
        P(),
    )
    return jax.shard_map(
        body,
        mesh=mesh,
        in_specs=placed,
        out_specs=(P(None, ("kvh", "seq")), P(None, ("kvh", "seq"))),
        check_vma=False,
    )
```

profile of v0, /device:TPU:0, one launch (start us, length us, event | category | flops | bytes accessed | tf_op | source)
XLA Modules:
  0.0 202.7 jit_solution(11224662813829926813)
XLA Ops:
  7.2 0.0 copy-start
  7.2 0.0 copy-start.1
  7.2 0.0 all-reduce.2.cloned.1.call-start
  7.2 0.8 iota_compare_fusion
  8.0 0.1 copy-done
  8.1 1.1 select_reduce_fusion
  9.2 15.8 %all-gather = f32[32,2,16]{2,1,0:T(2,128)S(1)} all-gather(f32[4,2,16]{2,1,0:T(2,128)S(1)} %get-tuple-element.201), channel_id=2, replica_groups=mesh['kvh'=4,'seq'=8] {'seq'}, dimensions={0}, use_global_device_ids=true | all-gather | bytes 4608 | tf_op jit(solution)/shard_map/all_gather | solution.py:8
  25.0 0.2 convert_reduce_fusion
  25.2 1.2 fusion.6
  26.4 14.8 %all-gather.2 = f32[32,2,16,128]{3,2,1,0:T(8,128)S(1)} all-gather(f32[4,2,16,128]{3,2,1,0:T(8,128)S(1)} %fusion.6), channel_id=4, replica_groups=mesh['kvh'=4,'seq'=8] {'seq'}, dimensions={0}, use_global_device_ids=true | all-gather | bytes 589824 | tf_op jit(solution)/shard_map/all_gather | solution.py:8
  41.2 14.2 %all-gather.1 = f32[32,2,16]{2,1,0:T(2,128)S(1)} all-gather(f32[4,2,16]{2,1,0:T(2,128)S(1)} %convert_reduce_fusion), channel_id=3, replica_groups=mesh['kvh'=4,'seq'=8] {'seq'}, dimensions={0}, use_global_device_ids=true | all-gather | bytes 4608 | tf_op jit(solution)/shard_map/all_gather | solution.py:8
  55.4 1.2 while.19
  55.4 0.1 fusion.17
  55.6 0.1 fusion.17
  55.7 0.1 fusion.17
  55.9 0.1 fusion.17
  56.1 0.1 fusion.17
  56.3 0.1 fusion.17
  56.4 0.1 fusion.17
  56.6 0.1 broadcast_divide_fusion
  56.7 8.8 %fusion.5 = f32[4,16384]{1,0:T(4,128)} fusion(bf16[512,16384]{1,0:T(8,128)(2,1)} %param.14, bf16[4,4096]{1,0:T(4,128)(2,1)S(1)} %bitcast.37, s32[]{:T(128)S(6)} %select_n.28), kind=kOutput, calls=%fused_computation.20 | convolution fusion | flops 67108864 | bytes 17043460 | tf_op jit(solution)/shard_map/dot_general | solution.py:48
  65.4 0.0 all-reduce.2.cloned.1.call-update
  65.5 0.8 dynamic-slice
  66.2 0.0 copy-done.1
  66.2 42.1 %all_gather.21 = bf16[4,16384]{1,0:T(4,128)(2,1)S(1)} all-gather(bf16[4,512]{1,0:T(4,128)(2,1)S(1)} %copy-done.1), channel_id=1, replica_groups=mesh['kvh'=4,'seq'=8] {'kvh','seq'}, dimensions={1}, use_global_device_ids=true | all-gather | bytes 135168 | tf_op jit(solution)/shard_map/all_gather | solution.py:53
  108.4 85.0 %all-reduce.2.cloned.1.call-done = f32[4,16384]{1,0:T(4,128)} async-done(((f32[4,16384]{1,0:T(4,128)}), f32[4,16384]{1,0:T(4,128)}) %all-reduce.2.cloned.1.call-update) | async-done | bytes 262160 | tf_op jit(solution)/shard_map/psum | solution.py:52
  193.4 1.2 multiply_reduce_fusion
  194.6 0.6 constant_dynamic-slice_fusion
  195.2 0.7 fusion.4
  (13 shorter events, 0.3 us)
Async XLA Ops:
  7.2 1.0 copy-start
  7.2 59.1 %copy-start.1 = (bf16[4,512]{1,0:T(4,128)(2,1)S(1)}, bf16[4,512]{1,0:T(4,128)(2,1)}, u32[]{:S(2)}) copy-start(bf16[4,512]{1,0:T(4,128)(2,1)} %param.13) | copy-start | bytes 12292
  7.2 186.2 %all-reduce.2.cloned.1.call-start = ((), (), s32[]{:S(2)}) async-start(), calls=%async_computation | async-start | bytes 524288 | tf_op jit(solution)/shard_map/psum | solution.py:52
Sparse Core Ops, SparseCore 0:
  65.6 127.7 all-reduce.1
where the time goes:
time: 203 us
  blocking collectives  86.9 us (43%)
  waiting for transfers between devices  85 us (42%)
  between operations  14.1 us (7%)
  matrix products  11 us (5%)
  other arithmetic  3.94 us (2%)
    psum x1, waiting for transfers between devices, body(): projected_all = lax.psum(projected, ('kvh', 'seq'))  85 us
    all_gather x3, blocking collectives, merged(): everything = jax.tree.map(lambda part: lax.all_gather(part, axis), shard)  44.8 us
    all_gather x1, blocking collectives, body(): residual = lax.all_gather(hidden_in, ('kvh', 'seq'), axis=1, tiled=True)  42.1 us
    dot_general x1, matrix products, body(): jnp.dot(attention, out_weight, preferred_element_type=jnp.float32)  8.75 us
  transfers between devices with their start and end apart: 1, of which 1 were waited for; matrix products, arithmetic and copies ran while one was open for 0% of the time, Pallas kernels for 0%

commit v1 on v0

--- a/solution.py
+++ b/solution.py
@@ -1,7 +1,214 @@
+import functools
+
 import jax
 import jax.numpy as jnp
 from jax import lax
+from jax.experimental import pallas as pl
+from jax.experimental.pallas import tpu as pltpu
 from jax.sharding import PartitionSpec as P
+
+MESH = pl.DeviceIdType.MESH
+LANES = 128
+
+
+def fused_kernel(dims, q_hbm, k_hbm, v_hbm, len_ref, hid_hbm, w_hbm, gain_ref, att_ref, norm_ref,
+                 qv, kv, vv, hv, wv, send_a, recv_a, out_a, send_b, recv_b, send_c, recv_c,
+                 in_sem, w_sem, sa_sem, ra_sem, sb_sem, rb_sem, sc_sem, rc_sem):
+    n_kvh, n_seq, rows, heads, hd, groups, positions, width = dims
+    n = n_kvh * n_seq
+    per_group = heads // groups
+    own_heads = width // hd
+    dests = per_group // own_heads
+    m = rows * own_heads
+    half = m // 2
+    quarter = LANES // 4
+    kvh, seq = lax.axis_index("kvh"), lax.axis_index("seq")
+
+    def peer(a, b):
+        return lax.rem(kvh + a, n_kvh), lax.rem(seq + b, n_seq)
+
+    seq_order = sorted(range(n_seq), key=lambda b: -min(b, n_seq - b))
+    order = [(a, b) for b in seq_order for a in list(range(1, n_kvh)) + [0]]
+
+    barrier = pltpu.get_barrier_semaphore()
+    for a, b in order:
+        if a or b:
+            pl.semaphore_signal(barrier, inc=1, device_id=peer(a, b), device_id_type=MESH)
+
+    loads = [pltpu.make_async_copy(s, d, in_sem.at[i]) for i, (s, d) in enumerate(
+        [(q_hbm, qv), (k_hbm, kv), (v_hbm, vv), (hid_hbm, hv)])]
+    for load in loads:
+        load.start()
+    w_loads = []
+    for slot, (a, b) in enumerate(order):
+        pa, pb = peer(a, b)
+        col = pl.multiple_of((pa * n_seq + pb) * width, width)
+        load = pltpu.make_async_copy(w_hbm.at[:, pl.ds(col, width)], wv.at[slot], w_sem.at[slot])
+        load.start()
+        w_loads.append(load)
+
+    loads[0].wait()
+    loads[1].wait()
+    loads[2].wait()
+    lane = lax.broadcasted_iota(jnp.int32, (per_group, LANES), 1)
+    position = lax.broadcasted_iota(jnp.int32, (per_group, positions), 1)
+    for g in range(groups):
+        stats = []
+        for r in range(rows):
+            scores = lax.dot_general(qv[r, g * per_group:(g + 1) * per_group, :], kv[r, g],
+                                     (((1,), (1,)), ((), ())),
+                                     preferred_element_type=jnp.float32) * hd ** (-0.5)
+            valid = position < len_ref[r, 0]
+            peak = jnp.max(jnp.where(valid, scores, -jnp.inf), axis=1, keepdims=True)
+            probs = jnp.exp(jnp.where(valid, scores - peak, -jnp.inf)).astype(jnp.bfloat16)
+            weight = jnp.sum(probs.astype(jnp.float32), axis=1, keepdims=True)
+            part = jnp.dot(probs, vv[r, g], preferred_element_type=jnp.float32)
+            stats.append((peak, weight))
+            for j in range(dests):
+                send_a[g * dests + j, r * own_heads:(r + 1) * own_heads, :] = (
+                    part[j * own_heads:(j + 1) * own_heads, :])
+        for rr in range(rows // 2):
+            low, high = stats[rr], stats[rr + rows // 2]
+            tile = jnp.where(lane < 2 * quarter,
+                             jnp.where(lane < quarter, low[0], low[1]),
+                             jnp.where(lane < 3 * quarter, high[0], high[1]))
+            for j in range(dests):
+                send_a[g * dests + j, m + rr * own_heads:m + (rr + 1) * own_heads, :] = (
+                    tile[j * own_heads:(j + 1) * own_heads, :])
+
+    pl.semaphore_wait(barrier, n - 1)
+    copies = []
+    for b in seq_order:
+        if b:
+            pa, pb = peer(0, b)
+            copy = pltpu.make_async_remote_copy(
+                src_ref=send_a.at[pb], dst_ref=recv_a.at[b], send_sem=sa_sem.at[b],
+                recv_sem=ra_sem.at[b], device_id=(pa, pb), device_id_type=MESH)
+            copy.start()
+            copies.append(copy)
+    recv_a[0] = send_a[seq]
+    for copy in copies:
+        copy.wait_recv()
+
+    tiles = [recv_a[b, m:m + half, :] for b in range(n_seq)]
+    top = functools.reduce(jnp.maximum, tiles)
+    scales = [jnp.exp(tile - top) for tile in tiles]
+    denom = functools.reduce(jnp.add, [
+        scale * pltpu.roll(tile, LANES - quarter, 1) for scale, tile in zip(scales, tiles)])
+    for h in range(2):
+        at = h * 2 * quarter
+        numer = functools.reduce(jnp.add, [
+            scales[b][:, at:at + 1] * recv_a[b, h * half:(h + 1) * half, :] for b in range(n_seq)])
+        out_a[h * half:(h + 1) * half, :] = numer / denom[:, at:at + 1]
+    attention = jnp.concatenate(
+        [out_a[pl.ds(i, rows, stride=own_heads), :] for i in range(own_heads)], axis=1
+    ).astype(jnp.bfloat16)
+
+    own = None
+    for slot, (a, b) in enumerate(order):
+        w_loads[slot].wait()
+        product = jnp.dot(attention, wv[slot], preferred_element_type=jnp.float32)
+        if a == 0 and b == 0:
+            own = product
+            continue
+        send_b[slot] = product.astype(send_b.dtype)
+        copy = pltpu.make_async_remote_copy(
+            src_ref=send_b.at[slot], dst_ref=recv_b.at[slot], send_sem=sb_sem.at[slot],
+            recv_sem=rb_sem.at[slot], device_id=peer(a, b), device_id_type=MESH)
+        copy.start()
+        copies.append(copy)
+    loads[3].wait()
+    total = own + hv[...].astype(jnp.float32)
+    for copy in copies[n_seq - 1:]:
+        copy.wait_recv()
+    for slot in range(n - 1):
+        total = total + recv_b[slot].astype(jnp.float32)
+    attended = total.astype(jnp.bfloat16)
+    att_ref[...] = attended
+    stream = attended.astype(jnp.float32)
+    squares = jnp.sum(stream * stream, axis=1, keepdims=True)
+    lane_one = lax.broadcasted_iota(jnp.int32, (1, LANES), 1)
+    packed = jnp.zeros((1, LANES), jnp.float32)
+    share = LANES // rows
+    for r in range(rows):
+        packed = jnp.where(lane_one // share == r, squares[r:r + 1, :], packed)
+    send_c[...] = packed
+    last = []
+    for slot, (a, b) in enumerate(order):
+        if a or b:
+            copy = pltpu.make_async_remote_copy(
+                src_ref=send_c, dst_ref=recv_c.at[slot], send_sem=sc_sem.at[slot],
+                recv_sem=rc_sem.at[slot], device_id=peer(a, b), device_id_type=MESH)
+            copy.start()
+            last.append(copy)
+    gain_wide = gain_ref[...].astype(jnp.float32)
+    for copy in last:
+        copy.wait_recv()
+    for slot in range(n - 1):
+        packed = packed + recv_c[slot]
+    scale = lax.rsqrt(packed / (n * width) + 1e-05)
+    for r in range(rows):
+        norm_ref[r:r + 1, :] = (
+            stream[r:r + 1, :] * scale[:, r * share:r * share + 1] * gain_wide
+        ).astype(jnp.bfloat16)
+    for copy in copies + last:
+        copy.wait_send()
+
+
+def fused_body(queries, keys, values, lengths, hidden_in, out_weight, norm_gain):
+    rows, heads, hd = queries.shape
+    groups, positions = keys.shape[1], keys.shape[2]
+    n_kvh, n_seq = lax.axis_size("kvh"), lax.axis_size("seq")
+    n = n_kvh * n_seq
+    width = hidden_in.shape[1]
+    own_heads = width // hd
+    m = rows * own_heads
+    message = m + m // 2
+    start = lax.axis_index(("kvh", "seq")) * width
+    gain = lax.dynamic_slice_in_dim(norm_gain, start, width, 0).reshape(1, width)
+    dims = (n_kvh, n_seq, rows, heads, hd, groups, positions, width)
+    anywhere = pl.BlockSpec(memory_space=pl.ANY)
+    vmem = pl.BlockSpec(memory_space=pltpu.VMEM)
+    out = jax.ShapeDtypeStruct((rows, width), jnp.bfloat16)
+    return pl.pallas_call(
+        functools.partial(fused_kernel, dims),
+        out_shape=(out, out),
+        in_specs=[anywhere, anywhere, anywhere, pl.BlockSpec(memory_space=pltpu.SMEM), anywhere,
+                  anywhere, vmem],
+        out_specs=(vmem, vmem),
+        scratch_shapes=[
+            pltpu.VMEM(queries.shape, queries.dtype),
+            pltpu.VMEM(keys.shape, keys.dtype),
+            pltpu.VMEM(values.shape, values.dtype),
+            pltpu.VMEM(hidden_in.shape, hidden_in.dtype),
+            pltpu.VMEM((n, out_weight.shape[0], width), out_weight.dtype),
+            pltpu.VMEM((n_seq, message, hd), jnp.float32),
+            pltpu.VMEM((n_seq, message, hd), jnp.float32),
+            pltpu.VMEM((m, hd), jnp.float32),
+            pltpu.VMEM((n, rows, width), jnp.bfloat16),
+            pltpu.VMEM((n, rows, width), jnp.bfloat16),
+            pltpu.VMEM((1, LANES), jnp.float32),
+            pltpu.VMEM((n, 1, LANES), jnp.float32),
+            pltpu.SemaphoreType.DMA((4,)),
+            pltpu.SemaphoreType.DMA((n,)),
+            pltpu.SemaphoreType.DMA((n_seq,)),
+            pltpu.SemaphoreType.DMA((n_seq,)),
+            pltpu.SemaphoreType.DMA((n,)),
+            pltpu.SemaphoreType.DMA((n,)),
+            pltpu.SemaphoreType.DMA((n,)),
+            pltpu.SemaphoreType.DMA((n,)),
+        ],
+        compiler_params=pltpu.CompilerParams(
+            collective_id=0, has_side_effects=True, vmem_limit_bytes=48 * 1024 * 1024),
+    )(queries, keys, values, lengths, hidden_in, out_weight, gain)
+
+
+def fits(queries, keys, hidden_in, out_weight):
+    rows, heads, hd = queries.shape
+    groups, width = keys.shape[1], hidden_in.shape[1]
+    return (hd == LANES and width % hd == 0 and (heads // groups) % max(width // hd, 1) == 0
+            and rows % 2 == 0 and (rows * (width // hd)) % 16 == 0 and LANES % rows == 0
+            and out_weight.shape[0] == width and out_weight.size * 2 <= 32 * 1024 * 1024)
 
 
 def merged(shard, axis, combine):
@@ -62,6 +269,11 @@
     return (attended, normed)
 
 
+def either_body(queries, keys, values, lengths, hidden_in, out_weight, norm_gain):
+    chosen = fused_body if fits(queries, keys, hidden_in, out_weight) else body
+    return chosen(queries, keys, values, lengths, hidden_in, out_weight, norm_gain)
+
+
 def solution(mesh):
     placed = (
         P(None, "kvh", None),
@@ -73,7 +285,7 @@
         P(),
     )
     return jax.shard_map(
-        body,
+        either_body,
         mesh=mesh,
         in_specs=placed,
         out_specs=(P(None, ("kvh", "seq")), P(None, ("kvh", "seq"))),

time: 203 us -> 34.3 us (0.17)
  blocking collectives: 86.9 us -> 0 us
  waiting for transfers between devices: 85 us -> 0 us
  Pallas kernels: 0 us -> 27.3 us
  between operations: 14.1 us -> 0.65 us
  matrix products: 11 us -> 0 us
  local copies, waits for them, and re-layouts: 1.53 us -> 6.04 us
  other arithmetic: 3.94 us -> 0 us
    all_gather x4 -> x0, blocking collectives: 86.9 us -> none  [the longest x3 44.8 us: merged(): everything = jax.tree.map(lambda part: lax.all_gather(part, axis), shard)]
    psum x1 -> x0, waiting for transfers between devices: 85 us -> none  [body(): projected_all = lax.psum(projected, ('kvh', 'seq'))]
    pallas_call x0 -> x1, Pallas kernels: none -> 27.3 us  [fused_body(): pl.pallas_call(functools.partial(fused_kernel, dims), out_shape=(out, out...]
    dot_general x3 -> x0, matrix products: 11 us -> none  [the longest x1 8.75 us: body(): jnp.dot(attention, out_weight, preferred_element_type=jnp.float32)]
    unnamed x5 -> x11, local copies, waits for them, and re-layouts: 0.15 us -> 5.27 us
  transfers between devices with their start and end apart: 1 -> 0, of which waited for: 1 -> 0; matrix products, arithmetic and copies ran while one was open for 0% -> 0% of each run, Pallas kernels for 0% -> 0%
where the time goes in v1:
time: 34.3 us; the launch traced here: 34 us
  Pallas kernels  27.3 us (80%)
  local copies, waits for them, and re-layouts  6.04 us (18%)
  between operations  0.65 us (2%)
    pallas_call x1, Pallas kernels, fused_body(): pl.pallas_call(functools.partial(fused_kernel, dims), out_shape=(out, out...  27.3 us
    unnamed x11, local copies, waits for them, and re-layouts  5.27 us
    dynamic_slice x1, local copies, waits for them, and re-layouts, fused_body(): lax.dynamic_slice_in_dim(norm_gain, start, width, 0).reshape(1, width)  0.76 us

profile of v1, /device:TPU:0, one launch (start us, length us, event | category | flops | bytes accessed | tf_op | source)
XLA Modules:
  0.0 34.0 jit_solution(12946083479937997170)
XLA Ops:
  0.6 0.8 %dynamic_slice.3 = bf16[512]{0:T(512)(128)(2,1)S(1)} dynamic-slice(bf16[16384]{0:T(1024)(128)(2,1)} %param.13, s32[]{:T(128)S(6)} %select_n.3), dynamic_slice_sizes={512} | dynamic-slice | bytes 2052 | tf_op jit(solution)/shard_map/dynamic_slice | solution.py:168
  1.4 0.7 %copy.9.len_ref = s32[4,1]{1,0:T(4,128)S(1)} copy(s32[4,1]{0,1:T(1,128)} %param.10) | data formatting | bytes 32 | tf_op args[3]
  2.1 0.0 copy-start
  2.1 0.9 %copy-done = bf16[4,2,128,128]{3,2,1,0:T(8,128)(2,1)S(1)} copy-done((bf16[4,2,128,128]{3,2,1,0:T(8,128)(2,1)S(1)}, bf16[4,2,128,128]{3,2,1,0:T(8,128)(2,1)}, u32[]{:S(2)}) %copy-start) | copy-done | bytes 262168
  3.1 0.0 copy-start.1
  3.1 0.9 %copy-done.1 = bf16[4,2,128,128]{3,2,1,0:T(8,128)(2,1)S(1)} copy-done((bf16[4,2,128,128]{3,2,1,0:T(8,128)(2,1)S(1)}, bf16[4,2,128,128]{3,2,1,0:T(8,128)(2,1)}, u32[]{:S(2)}) %copy-start.1) | copy-done | bytes 262168
  4.0 0.0 copy-start.2
  4.0 0.8 %copy-done.2 = bf16[4,32,128]{2,1,0:T(8,128)(2,1)S(1)} copy-done((bf16[4,32,128]{2,1,0:T(8,128)(2,1)S(1)}, bf16[4,32,128]{2,1,0:T(8,128)(2,1)}, u32[]{:S(2)}) %copy-start.2) | copy-done | bytes 32792
  4.8 0.0 copy-start.3
  4.8 0.7 %copy-done.3 = bf16[4,512]{1,0:T(4,128)(2,1)S(1)} copy-done((bf16[4,512]{1,0:T(4,128)(2,1)S(1)}, bf16[4,512]{1,0:T(4,128)(2,1)}, u32[]{:S(2)}) %copy-start.3) | copy-done | bytes 4120
  5.5 27.3 %shard_map.86 = (bf16[4,512]{1,0:T(4,128)(2,1)S(1)}, bf16[4,512]{1,0:T(4,128)(2,1)S(1)}) custom-call(bf16[4,32,128]{2,1,0:T(8,128)(2,1)S(1)} %copy-done.2, bf16[4,2,128,128]{3,2,1,0:T(8,128)(2,1)S(1)} %copy-done, bf16[4,2,128,128]{3,2,1,0:T(8,128)(2,1)S(1)} %copy-done.1, s32[4,1]{1,0:T(4,128)S(1)} %copy.9.len_ref, bf16[4,512]{1,0:T(4,128)(2,1)S(1)} %copy-done.3, ...), custom_call_target="tpu_custom_call" | custom-call | tf_op jit(solution)/shard_map/pallas_call | solution.py:173
  32.8 0.6 %copy.12 = bf16[4,512]{1,0:T(4,128)(2,1)} copy(bf16[4,512]{1,0:T(4,128)(2,1)S(1)} %get-tuple-element.4) | data formatting | bytes 8192
  33.4 0.6 %copy.13 = bf16[4,512]{1,0:T(4,128)(2,1)} copy(bf16[4,512]{1,0:T(4,128)(2,1)S(1)} %get-tuple-element.5) | data formatting | bytes 8192
  (1 shorter events, 0.0 us)
Async XLA Ops:
  2.1 0.9 %copy-start = (bf16[4,2,128,128]{3,2,1,0:T(8,128)(2,1)S(1)}, bf16[4,2,128,128]{3,2,1,0:T(8,128)(2,1)}, u32[]{:S(2)}) copy-start(bf16[4,2,128,128]{3,2,1,0:T(8,128)(2,1)} %k_hbm.1) | copy-start | bytes 786436
  3.1 0.9 %copy-start.1 = (bf16[4,2,128,128]{3,2,1,0:T(8,128)(2,1)S(1)}, bf16[4,2,128,128]{3,2,1,0:T(8,128)(2,1)}, u32[]{:S(2)}) copy-start(bf16[4,2,128,128]{3,2,1,0:T(8,128)(2,1)} %v_hbm.1) | copy-start | bytes 786436
  4.0 0.8 %copy-start.2 = (bf16[4,32,128]{2,1,0:T(8,128)(2,1)S(1)}, bf16[4,32,128]{2,1,0:T(8,128)(2,1)}, u32[]{:S(2)}) copy-start(bf16[4,32,128]{2,1,0:T(8,128)(2,1)} %q_hbm.1) | copy-start | bytes 98308
  4.8 0.7 %copy-start.3 = (bf16[4,512]{1,0:T(4,128)(2,1)S(1)}, bf16[4,512]{1,0:T(4,128)(2,1)}, u32[]{:S(2)}) copy-start(bf16[4,512]{1,0:T(4,128)(2,1)} %hid_hbm.1) | copy-start | bytes 12292

commit v2 on v1

--- a/solution.py
+++ b/solution.py
@@ -11,8 +11,8 @@
 LANES = 128
 
 
-def fused_kernel(dims, q_hbm, k_hbm, v_hbm, len_ref, hid_hbm, w_hbm, gain_ref, att_ref, norm_ref,
-                 qv, kv, vv, hv, wv, send_a, recv_a, out_a, send_b, recv_b, send_c, recv_c,
+def fused_kernel(dims, q_hbm, k_hbm, v_hbm, len_ref, hid_hbm, w_hbm, gain_hbm, out_ref,
+                 qv, kv, vv, hv, gv, wv, send_a, recv_a, out_a, send_b, recv_b, send_c, recv_c,
                  in_sem, w_sem, sa_sem, ra_sem, sb_sem, rb_sem, sc_sem, rc_sem):
     n_kvh, n_seq, rows, heads, hd, groups, positions, width = dims
     n = n_kvh * n_seq
@@ -24,11 +24,19 @@
     quarter = LANES // 4
     kvh, seq = lax.axis_index("kvh"), lax.axis_index("seq")
 
+    def flip(index, mask):
+        bits = mask.bit_length()
+        low = sum(lax.rem(index // (1 << i) + (mask >> i & 1), 2) * (1 << i) for i in range(bits))
+        return (index // (1 << bits)) * (1 << bits) + low
+
     def peer(a, b):
-        return lax.rem(kvh + a, n_kvh), lax.rem(seq + b, n_seq)
-
-    seq_order = sorted(range(n_seq), key=lambda b: -min(b, n_seq - b))
-    order = [(a, b) for b in seq_order for a in list(range(1, n_kvh)) + [0]]
+        return flip(kvh, a), flip(seq, b)
+
+    def hops(pair):
+        return (pair[0].bit_count() + (pair[1] >> 1)), pair[0], pair[1]
+
+    order = sorted(((a, b) for a in range(n_kvh) for b in range(n_seq)), key=hops, reverse=True)
+    seq_order = sorted(range(n_seq), reverse=True)
 
     barrier = pltpu.get_barrier_semaphore()
     for a, b in order:
@@ -36,7 +44,8 @@
             pl.semaphore_signal(barrier, inc=1, device_id=peer(a, b), device_id_type=MESH)
 
     loads = [pltpu.make_async_copy(s, d, in_sem.at[i]) for i, (s, d) in enumerate(
-        [(q_hbm, qv), (k_hbm, kv), (v_hbm, vv), (hid_hbm, hv)])]
+        [(q_hbm, qv), (k_hbm, kv), (v_hbm, vv), (hid_hbm, hv),
+         (gain_hbm.at[pl.ds(pl.multiple_of((kvh * n_seq + seq) * width, width), width)], gv)])]
     for load in loads:
         load.start()
     w_loads = []
@@ -58,7 +67,7 @@
             scores = lax.dot_general(qv[r, g * per_group:(g + 1) * per_group, :], kv[r, g],
                                      (((1,), (1,)), ((), ())),
                                      preferred_element_type=jnp.float32) * hd ** (-0.5)
-            valid = position < len_ref[r, 0]
+            valid = position < len_ref[0, r]
             peak = jnp.max(jnp.where(valid, scores, -jnp.inf), axis=1, keepdims=True)
             probs = jnp.exp(jnp.where(valid, scores - peak, -jnp.inf)).astype(jnp.bfloat16)
             weight = jnp.sum(probs.astype(jnp.float32), axis=1, keepdims=True)
@@ -119,12 +128,14 @@
         copies.append(copy)
     loads[3].wait()
     total = own + hv[...].astype(jnp.float32)
-    for copy in copies[n_seq - 1:]:
-        copy.wait_recv()
-    for slot in range(n - 1):
-        total = total + recv_b[slot].astype(jnp.float32)
+    for first in range(0, n - 1, 8):
+        group = range(first, min(first + 8, n - 1))
+        for slot in group:
+            copies[n_seq - 1 + slot].wait_recv()
+        for slot in group:
+            total = total + recv_b[slot].astype(jnp.float32)
     attended = total.astype(jnp.bfloat16)
-    att_ref[...] = attended
+    out_ref[0] = attended
     stream = attended.astype(jnp.float32)
     squares = jnp.sum(stream * stream, axis=1, keepdims=True)
     lane_one = lax.broadcasted_iota(jnp.int32, (1, LANES), 1)
@@ -141,14 +152,15 @@
                 recv_sem=rc_sem.at[slot], device_id=peer(a, b), device_id_type=MESH)
             copy.start()
             last.append(copy)
-    gain_wide = gain_ref[...].astype(jnp.float32)
+    loads[4].wait()
+    gain_wide = gv[...].astype(jnp.float32).reshape(1, width)
     for copy in last:
         copy.wait_recv()
     for slot in range(n - 1):
         packed = packed + recv_c[slot]
     scale = lax.rsqrt(packed / (n * width) + 1e-05)
     for r in range(rows):
-        norm_ref[r:r + 1, :] = (
+        out_ref[1, r:r + 1, :] = (
             stream[r:r + 1, :] * scale[:, r * share:r * share + 1] * gain_wide
         ).astype(jnp.bfloat16)
     for copy in copies + last:
@@ -164,23 +176,20 @@
     own_heads = width // hd
     m = rows * own_heads
     message = m + m // 2
-    start = lax.axis_index(("kvh", "seq")) * width
-    gain = lax.dynamic_slice_in_dim(norm_gain, start, width, 0).reshape(1, width)
     dims = (n_kvh, n_seq, rows, heads, hd, groups, positions, width)
-    anywhere = pl.BlockSpec(memory_space=pl.ANY)
+    hbm = pl.BlockSpec(memory_space=pltpu.HBM)
     vmem = pl.BlockSpec(memory_space=pltpu.VMEM)
-    out = jax.ShapeDtypeStruct((rows, width), jnp.bfloat16)
-    return pl.pallas_call(
+    both = pl.pallas_call(
         functools.partial(fused_kernel, dims),
-        out_shape=(out, out),
-        in_specs=[anywhere, anywhere, anywhere, pl.BlockSpec(memory_space=pltpu.SMEM), anywhere,
-                  anywhere, vmem],
-        out_specs=(vmem, vmem),
+        out_shape=jax.ShapeDtypeStruct((2, rows, width), jnp.bfloat16),
+        in_specs=[hbm, hbm, hbm, pl.BlockSpec(memory_space=pltpu.SMEM), hbm, hbm, hbm],
+        out_specs=vmem,
         scratch_shapes=[
             pltpu.VMEM(queries.shape, queries.dtype),
             pltpu.VMEM(keys.shape, keys.dtype),
             pltpu.VMEM(values.shape, values.dtype),
             pltpu.VMEM(hidden_in.shape, hidden_in.dtype),
+            pltpu.VMEM((width,), norm_gain.dtype),
             pltpu.VMEM((n, out_weight.shape[0], width), out_weight.dtype),
             pltpu.VMEM((n_seq, message, hd), jnp.float32),
             pltpu.VMEM((n_seq, message, hd), jnp.float32),
@@ -189,7 +198,7 @@
             pltpu.VMEM((n, rows, width), jnp.bfloat16),
             pltpu.VMEM((1, LANES), jnp.float32),
             pltpu.VMEM((n, 1, LANES), jnp.float32),
-            pltpu.SemaphoreType.DMA((4,)),
+            pltpu.SemaphoreType.DMA((5,)),
             pltpu.SemaphoreType.DMA((n,)),
             pltpu.SemaphoreType.DMA((n_seq,)),
             pltpu.SemaphoreType.DMA((n_seq,)),
@@ -199,14 +208,16 @@
             pltpu.SemaphoreType.DMA((n,)),
         ],
         compiler_params=pltpu.CompilerParams(
-            collective_id=0, has_side_effects=True, vmem_limit_bytes=48 * 1024 * 1024),
-    )(queries, keys, values, lengths, hidden_in, out_weight, gain)
+            collective_id=0, has_side_effects=True, vmem_limit_bytes=67043328),
+    )(queries, keys, values, lengths.T, hidden_in, out_weight, norm_gain)
+    return both[0], both[1]
 
 
 def fits(queries, keys, hidden_in, out_weight):
     rows, heads, hd = queries.shape
     groups, width = keys.shape[1], hidden_in.shape[1]
-    return (hd == LANES and width % hd == 0 and (heads // groups) % max(width // hd, 1) == 0
+    n_kvh, n_seq = lax.axis_size("kvh"), lax.axis_size("seq")
+    return (hd == LANES and n_kvh & (n_kvh - 1) == 0 and n_seq & (n_seq - 1) == 0 and width % hd == 0 and (heads // groups) % max(width // hd, 1) == 0
             and rows % 2 == 0 and (rows * (width // hd)) % 16 == 0 and LANES % rows == 0
             and out_weight.shape[0] == width and out_weight.size * 2 <= 32 * 1024 * 1024)
 

time: 34.3 us -> 33.6 us (0.980)
  local copies, waits for them, and re-layouts: 6.04 us -> 1.28 us
  Pallas kernels: 27.3 us -> 31.5 us
    unnamed x11 -> x0, local copies, waits for them, and re-layouts: 5.27 us -> none
    pallas_call x1, Pallas kernels: 27.3 us -> 31.5 us  [fused_body(): pl.pallas_call(functools.partial(fused_kernel, dims), out_shape=jax.Shape...]
    squeeze x0 -> x1, local copies, waits for them, and re-layouts: none -> 1.28 us  [fused_body(): return (both[0], both[1])]
    dynamic_slice x1 -> x0, local copies, waits for them, and re-layouts: 0.76 us -> none  [fused_body(): lax.dynamic_slice_in_dim(norm_gain, start, width, 0).reshape(1, width)]
where the time goes in v2:
time: 33.6 us; the launch traced here: 33.4 us
  Pallas kernels  31.5 us (94%)
  local copies, waits for them, and re-layouts  1.28 us (4%)
  between operations  0.64 us (2%)
    pallas_call x1, Pallas kernels, fused_body(): pl.pallas_call(functools.partial(fused_kernel, dims), out_shape=jax.Shape...  31.5 us
    squeeze x1, local copies, waits for them, and re-layouts, fused_body(): return (both[0], both[1])  1.28 us

profile of v2, /device:TPU:0, one launch (start us, length us, event | category | flops | bytes accessed | tf_op | source)
XLA Modules:
  0.0 33.4 jit_solution(5019781873320527826)
XLA Ops:
  0.6 31.5 %shard_map.86 = bf16[2,4,512]{2,1,0:T(4,128)(2,1)} custom-call(bf16[4,32,128]{2,1,0:T(8,128)(2,1)} %q_hbm.1, bf16[4,2,128,128]{3,2,1,0:T(8,128)(2,1)} %k_hbm.1, bf16[4,2,128,128]{3,2,1,0:T(8,128)(2,1)} %v_hbm.1, s32[1,4]{1,0:T(1,128)} %bitcast.5, bf16[4,512]{1,0:T(4,128)(2,1)} %hid_hbm.1, bf16[512,16384]{1,0:T(8,128)(2,1)} %w_hbm.1, bf16[16384]{0:T(1024)(128)(2,1)} %gain_hbm.1), custom_call_target="tpu_custom_call" | custom-call | tf_op jit(solution)/shard_map/pallas_call | solution.py:182
  32.1 1.3 %slice_bitcast_fusion = (bf16[4,512]{1,0:T(4,128)(2,1)}, bf16[4,512]{1,0:T(4,128)(2,1)}) fusion(bf16[2,4,512]{2,1,0:T(4,128)(2,1)} %shard_map.86), kind=kLoop, calls=%fused_computation | loop fusion | bytes 16384 | tf_op jit(solution)/shard_map/squeeze | solution.py:213

commit v3 on v2

--- a/solution.py
+++ b/solution.py
@@ -9,10 +9,11 @@
 
 MESH = pl.DeviceIdType.MESH
 LANES = 128
-
-
-def fused_kernel(dims, q_hbm, k_hbm, v_hbm, len_ref, hid_hbm, w_hbm, gain_hbm, out_ref,
-                 qv, kv, vv, hv, gv, wv, send_a, recv_a, out_a, send_b, recv_b, send_c, recv_c,
+CHUNK = 4
+
+
+def fused_kernel(dims, q_hbm, k_hbm, v_hbm, len_hbm, hid_hbm, w_hbm, gain_hbm, out_ref,
+                 qv, kv, vv, lv, hv, gv, wv, send_a, recv_a, out_a, send_b, recv_b, send_c, recv_c,
                  in_sem, w_sem, sa_sem, ra_sem, sb_sem, rb_sem, sc_sem, rc_sem):
     n_kvh, n_seq, rows, heads, hd, groups, positions, width = dims
     n = n_kvh * n_seq
@@ -38,15 +39,17 @@
     order = sorted(((a, b) for a in range(n_kvh) for b in range(n_seq)), key=hops, reverse=True)
     seq_order = sorted(range(n_seq), reverse=True)
 
+    loads = [pltpu.make_async_copy(s, d, in_sem.at[i]) for i, (s, d) in enumerate(
+        [(q_hbm, qv), (k_hbm, kv), (v_hbm, vv), (len_hbm, lv), (hid_hbm, hv),
+         (gain_hbm.at[pl.ds(pl.multiple_of((kvh * n_seq + seq) * width, width), width)], gv)])]
+    for load in loads[:4]:
+        load.start()
     barrier = pltpu.get_barrier_semaphore()
     for a, b in order:
         if a or b:
             pl.semaphore_signal(barrier, inc=1, device_id=peer(a, b), device_id_type=MESH)
 
-    loads = [pltpu.make_async_copy(s, d, in_sem.at[i]) for i, (s, d) in enumerate(
-        [(q_hbm, qv), (k_hbm, kv), (v_hbm, vv), (hid_hbm, hv),
-         (gain_hbm.at[pl.ds(pl.multiple_of((kvh * n_seq + seq) * width, width), width)], gv)])]
-    for load in loads:
+    for load in loads[4:]:
         load.start()
     w_loads = []
     for slot, (a, b) in enumerate(order):
@@ -56,9 +59,8 @@
         load.start()
         w_loads.append(load)
 
-    loads[0].wait()
-    loads[1].wait()
-    loads[2].wait()
+    for load in loads[:4]:
+        load.wait()
     lane = lax.broadcasted_iota(jnp.int32, (per_group, LANES), 1)
     position = lax.broadcasted_iota(jnp.int32, (per_group, positions), 1)
     for g in range(groups):
@@ -67,7 +69,7 @@
             scores = lax.dot_general(qv[r, g * per_group:(g + 1) * per_group, :], kv[r, g],
                                      (((1,), (1,)), ((), ())),
                                      preferred_element_type=jnp.float32) * hd ** (-0.5)
-            valid = position < len_ref[0, r]
+            valid = position < lv[0:1, r:r + 1]
             peak = jnp.max(jnp.where(valid, scores, -jnp.inf), axis=1, keepdims=True)
             probs = jnp.exp(jnp.where(valid, scores - peak, -jnp.inf)).astype(jnp.bfloat16)
             weight = jnp.sum(probs.astype(jnp.float32), axis=1, keepdims=True)
@@ -113,20 +115,24 @@
         [out_a[pl.ds(i, rows, stride=own_heads), :] for i in range(own_heads)], axis=1
     ).astype(jnp.bfloat16)
 
-    own = None
-    for slot, (a, b) in enumerate(order):
-        w_loads[slot].wait()
-        product = jnp.dot(attention, wv[slot], preferred_element_type=jnp.float32)
-        if a == 0 and b == 0:
-            own = product
-            continue
-        send_b[slot] = product.astype(send_b.dtype)
-        copy = pltpu.make_async_remote_copy(
-            src_ref=send_b.at[slot], dst_ref=recv_b.at[slot], send_sem=sb_sem.at[slot],
-            recv_sem=rb_sem.at[slot], device_id=peer(a, b), device_id_type=MESH)
-        copy.start()
-        copies.append(copy)
-    loads[3].wait()
+    for first in range(0, n, CHUNK):
+        slots = range(first, first + CHUNK)
+        for slot in slots:
+            w_loads[slot].wait()
+        products = [jnp.dot(attention, wv[slot], preferred_element_type=jnp.float32)
+                    for slot in slots]
+        for slot, product in zip(slots, products):
+            if slot < n - 1:
+                send_b[slot] = product.astype(send_b.dtype)
+        for slot in slots:
+            if slot < n - 1:
+                copy = pltpu.make_async_remote_copy(
+                    src_ref=send_b.at[slot], dst_ref=recv_b.at[slot], send_sem=sb_sem.at[slot],
+                    recv_sem=rb_sem.at[slot], device_id=peer(*order[slot]), device_id_type=MESH)
+                copy.start()
+                copies.append(copy)
+    own = products[-1]
+    loads[4].wait()
     total = own + hv[...].astype(jnp.float32)
     for first in range(0, n - 1, 8):
         group = range(first, min(first + 8, n - 1))
@@ -152,7 +158,7 @@
                 recv_sem=rc_sem.at[slot], device_id=peer(a, b), device_id_type=MESH)
             copy.start()
             last.append(copy)
-    loads[4].wait()
+    loads[5].wait()
     gain_wide = gv[...].astype(jnp.float32).reshape(1, width)
     for copy in last:
         copy.wait_recv()
@@ -182,12 +188,13 @@
     both = pl.pallas_call(
         functools.partial(fused_kernel, dims),
         out_shape=jax.ShapeDtypeStruct((2, rows, width), jnp.bfloat16),
-        in_specs=[hbm, hbm, hbm, pl.BlockSpec(memory_space=pltpu.SMEM), hbm, hbm, hbm],
+        in_specs=[hbm] * 7,
         out_specs=vmem,
         scratch_shapes=[
             pltpu.VMEM(queries.shape, queries.dtype),
             pltpu.VMEM(keys.shape, keys.dtype),
             pltpu.VMEM(values.shape, values.dtype),
+            pltpu.VMEM(lengths.T.shape, lengths.dtype),
             pltpu.VMEM(hidden_in.shape, hidden_in.dtype),
             pltpu.VMEM((width,), norm_gain.dtype),
             pltpu.VMEM((n, out_weight.shape[0], width), out_weight.dtype),
@@ -198,7 +205,7 @@
             pltpu.VMEM((n, rows, width), jnp.bfloat16),
             pltpu.VMEM((1, LANES), jnp.float32),
             pltpu.VMEM((n, 1, LANES), jnp.float32),
-            pltpu.SemaphoreType.DMA((5,)),
+            pltpu.SemaphoreType.DMA((6,)),
             pltpu.SemaphoreType.DMA((n,)),
             pltpu.SemaphoreType.DMA((n_seq,)),
             pltpu.SemaphoreType.DMA((n_seq,)),
@@ -217,7 +224,7 @@
     rows, heads, hd = queries.shape
     groups, width = keys.shape[1], hidden_in.shape[1]
     n_kvh, n_seq = lax.axis_size("kvh"), lax.axis_size("seq")
-    return (hd == LANES and n_kvh & (n_kvh - 1) == 0 and n_seq & (n_seq - 1) == 0 and width % hd == 0 and (heads // groups) % max(width // hd, 1) == 0
+    return (hd == LANES and n_kvh & (n_kvh - 1) == 0 and n_seq & (n_seq - 1) == 0 and n_kvh * n_seq % CHUNK == 0 and width % hd == 0 and (heads // groups) % max(width // hd, 1) == 0
             and rows % 2 == 0 and (rows * (width // hd)) % 16 == 0 and LANES % rows == 0
             and out_weight.shape[0] == width and out_weight.size * 2 <= 32 * 1024 * 1024)
 

time: 33.6 us -> 25.7 us (0.76)
  Pallas kernels: 31.5 us -> 23.6 us
    pallas_call x1, Pallas kernels: 31.5 us -> 23.6 us  [fused_body(): pl.pallas_call(functools.partial(fused_kernel, dims), out_shape=jax.Shape...]
where the time goes in v3:
time: 25.7 us; the launch traced here: 25.5 us
  Pallas kernels  23.6 us (92%)
  local copies, waits for them, and re-layouts  1.28 us (5%)
  between operations  0.64 us (2%)
    pallas_call x1, Pallas kernels, fused_body(): pl.pallas_call(functools.partial(fused_kernel, dims), out_shape=jax.Shape...  23.6 us
    squeeze x1, local copies, waits for them, and re-layouts, fused_body(): return (both[0], both[1])  1.28 us

profile of v3, /device:TPU:0, one launch (start us, length us, event | category | flops | bytes accessed | tf_op | source)
XLA Modules:
  0.0 25.5 jit_solution(9474478197812340121)
XLA Ops:
  0.6 23.6 %shard_map.86 = bf16[2,4,512]{2,1,0:T(4,128)(2,1)} custom-call(bf16[4,32,128]{2,1,0:T(8,128)(2,1)} %q_hbm.1, bf16[4,2,128,128]{3,2,1,0:T(8,128)(2,1)} %k_hbm.1, bf16[4,2,128,128]{3,2,1,0:T(8,128)(2,1)} %v_hbm.1, s32[1,4]{1,0:T(1,128)} %bitcast.5, bf16[4,512]{1,0:T(4,128)(2,1)} %hid_hbm.1, bf16[512,16384]{1,0:T(8,128)(2,1)} %w_hbm.1, bf16[16384]{0:T(1024)(128)(2,1)} %gain_hbm.1), custom_call_target="tpu_custom_call" | custom-call | tf_op jit(solution)/shard_map/pallas_call | solution.py:188
  24.2 1.3 %slice_bitcast_fusion = (bf16[4,512]{1,0:T(4,128)(2,1)}, bf16[4,512]{1,0:T(4,128)(2,1)}) fusion(bf16[2,4,512]{2,1,0:T(4,128)(2,1)} %shard_map.86), kind=kLoop, calls=%fused_computation | loop fusion | bytes 16384 | tf_op jit(solution)/shard_map/squeeze | solution.py:220

commit v4 on v3

--- a/solution.py
+++ b/solution.py
@@ -215,8 +215,9 @@
             pltpu.SemaphoreType.DMA((n,)),
         ],
         compiler_params=pltpu.CompilerParams(
-            collective_id=0, has_side_effects=True, vmem_limit_bytes=67043328),
-    )(queries, keys, values, lengths.T, hidden_in, out_weight, norm_gain)
+            collective_id=0, has_side_effects=True, vmem_limit_bytes=40 * 1024 * 1024),
+    )(*(pltpu.with_memory_space_constraint(operand, pltpu.HBM) for operand in (
+        queries, keys, values, lengths.T, hidden_in, out_weight, norm_gain)))
     return both[0], both[1]
 
 

time: 25.7 us -> 24.4 us (0.949)
  local copies, waits for them, and re-layouts: 1.28 us -> 0.6 us
  Pallas kernels: 23.6 us -> 23 us
    squeeze x1, local copies, waits for them, and re-layouts: 1.28 us -> 0.6 us  [fused_body(): return (both[0], both[1])]
    pallas_call x1, Pallas kernels: 23.6 us -> 23 us  [fused_body(): pl.pallas_call(functools.partial(fused_kernel, dims), out_shape=jax.Shape...]
where the time goes in v4:
time: 24.4 us; the launch traced here: 24.3 us
  Pallas kernels  23 us (94%)
  between operations  0.64 us (3%)
  local copies, waits for them, and re-layouts  0.6 us (2%)
    pallas_call x1, Pallas kernels, fused_body(): pl.pallas_call(functools.partial(fused_kernel, dims), out_shape=jax.Shape...  23 us
    squeeze x1, local copies, waits for them, and re-layouts, fused_body(): return (both[0], both[1])  0.6 us

profile of v4, /device:TPU:0, one launch (start us, length us, event | category | flops | bytes accessed | tf_op | source)
XLA Modules:
  0.0 24.3 jit_solution(1927117145023951247)
XLA Ops:
  0.6 23.0 %shard_map.86 = bf16[2,4,512]{2,1,0:T(4,128)(2,1)S(1)} custom-call(bf16[4,32,128]{2,1,0:T(8,128)(2,1)} %q_hbm.1, bf16[4,2,128,128]{3,2,1,0:T(8,128)(2,1)} %k_hbm.1, bf16[4,2,128,128]{3,2,1,0:T(8,128)(2,1)} %v_hbm.1, s32[1,4]{1,0:T(1,128)} %bitcast.5, bf16[4,512]{1,0:T(4,128)(2,1)} %hid_hbm.1, bf16[512,16384]{1,0:T(8,128)(2,1)} %w_hbm.1, ...), custom_call_target="tpu_custom_call" | custom-call | tf_op jit(solution)/shard_map/pallas_call | solution.py:188
  23.7 0.6 %slice_bitcast_fusion = (bf16[4,512]{1,0:T(4,128)(2,1)}, bf16[4,512]{1,0:T(4,128)(2,1)}) fusion(bf16[2,4,512]{2,1,0:T(4,128)(2,1)S(1)} %shard_map.86), kind=kLoop, calls=%fused_computation | loop fusion | bytes 16384 | tf_op jit(solution)/shard_map/squeeze | solution.py:221
